TPU v7x, 512 devices: a whole 4x8x8 slice. The times are simulated.
512 devices in a mesh: pb: 32 (over z, x), ka: 16 (over y, core).
Axes of the slice: x: 4, y: 8, z: 8, core: 2. Of those that a mesh axis runs over, the one named last changes fastest.
Arguments:
- features: bfloat16 [65536, 1024], P(('pb', 'ka')), may hold values from -8.5 to 8.5
- order: int32 [65536], P(('pb', 'ka')), may hold values from 0 to 127, as said below
- neighbours: int32 [512, 24], P('pb'), may hold values from 0 to 511, as said below
- counts: int32 [512], P('pb'), may hold values from 1 to 24, as said below
- qkv_weight: bfloat16 [1024, 1536], P(('pb', 'ka')), may hold values from -0.25 to 0.25
- out_weight: bfloat16 [512, 1024], P(None, ('pb', 'ka')), may hold values from -1 to 1
Outputs:
- mixed: bfloat16 [65536, 1024], P(('pb', 'ka'))
Inputs may be any that keep to these rules, and one draw needn't show every extreme that they name: `order`: each aligned group of 128 entries is a permutation of 0 to 127. `neighbours`: entry 0 of the list of block a is a itself; the first counts[a] entries are distinct and lie in a's slab of 16 blocks or in the slabs just before and after it, cyclically; slots from counts[a] on hold some block id and are not part of the list. `counts`: some block's list fills all 24 slots.
All inputs are finite; a program needn't handle non-finite values.
Results may differ from a plain program's by a relative error of at most 0.012.
The roundings to bfloat16 on the way count: a program that leaves them out, or rounds other values in their place, can miss the bound.
Values may be sent and summed in bfloat16 or wider, within the bound.
No kernel may reach another device: no remote copies, remote signals or barrier semaphores. Data moves between devices by JAX's collectives and lax.ppermute only.
A program may use at most 64 MiB of HBM per device.

v0:
```python
import jax
import jax.numpy as jnp
from jax import lax
from jax.sharding import PartitionSpec as P

HD = 64
BLK = 128


def padded(array, sides, width):
    for axis, dim in sides:
        size, length = (lax.axis_size(axis), array.shape[dim])
        up = [(i, (i + 1) % size) for i in range(size)]
        down = [(j, i) for i, j in up]
        last = lax.slice_in_dim(array, length - width, length, axis=dim)
        leading = lax.slice_in_dim(array, 0, width, axis=dim)
        before = lax.ppermute(last, axis, up)
        after = lax.ppermute(leading, axis, down)
        array = jnp.concatenate([before, array, after], axis=dim)
    return array


def attend_rows(query_rows, allow_rows, near_keys, near_values, score_scale):
    row_total = query_rows.shape[0]
    head_count = query_rows.shape[1]
    attn_width = head_count * query_rows.shape[2]
    tile_rows = 512
    tile_count = row_total // tile_rows

    def attend(tile_args):
        query_tile, allow_tile = tile_args
        allowed = jnp.repeat(allow_tile, BLK, axis=1)
        scores = (
            jnp.einsum("qhd,khd->hqk", query_tile, near_keys, preferred_element_type=jnp.float32)
            * score_scale
        )
        row_max = jnp.max(jnp.where(allowed[None], scores, -1e30), axis=-1)
        row_shift = row_max.astype(jnp.bfloat16)
        soft_weights = jnp.where(
            allowed[None], jnp.exp(scores - row_shift.astype(jnp.float32)[..., None]), 0.0
        )
        group_total = jnp.sum(soft_weights, axis=-1).T
        numerator = jnp.einsum(
            "hqk,khd->qhd",
            soft_weights.astype(jnp.bfloat16),
            near_values,
            preferred_element_type=jnp.float32,
        )
        positive = group_total > 0
        partial_value = jnp.where(
            positive[..., None], numerator / jnp.where(positive, group_total, 1.0)[..., None], 0.0
        )
        return (
            partial_value.astype(jnp.bfloat16).reshape(tile_rows, attn_width),
            row_shift.T,
            group_total.astype(jnp.bfloat16),
        )

    tiled = lax.map(
        attend,
        (
            query_rows.reshape(tile_count, tile_rows, head_count, query_rows.shape[2]),
            allow_rows.reshape(tile_count, tile_rows, -1),
        ),
    )
    return (
        tiled[0].reshape(row_total, attn_width),
        tiled[1].reshape(row_total, head_count),
        tiled[2].reshape(row_total, head_count),
    )


def body(features, order, neighbours, counts, qkv_weight, out_weight):
    dev_rows = features.shape[0]
    sorted_rows = jnp.take(features, order, axis=0)
    attn_width = qkv_weight.shape[1] // 3
    head_count = attn_width // HD
    score_scale = HD ** (-0.5)
    projected = jnp.dot(
        sorted_rows,
        lax.all_gather(qkv_weight, ("pb", "ka"), axis=0, tiled=True),
        preferred_element_type=jnp.float32,
    )
    own_queries = projected[:, :attn_width].astype(jnp.bfloat16)
    keys_values = projected[:, attn_width:].astype(jnp.bfloat16)
    near = padded(keys_values, (("pb", 0),), dev_rows)
    slab_index = lax.axis_index("pb")
    group_index = lax.axis_index("ka")
    slab_count = lax.axis_size("pb")
    group_count = lax.axis_size("ka")
    dev_blocks = dev_rows // BLK
    slab_of = (slab_index + jnp.arange(3) - 1) % slab_count
    listed_slot = jnp.arange(neighbours.shape[1])[None, :] < counts[:, None]
    slab_queries = lax.all_gather(own_queries, "ka", axis=0, tiled=True)
    near_keys = near[:, :attn_width].reshape(3 * dev_rows, head_count, HD)
    near_values = near[:, attn_width:].reshape(3 * dev_rows, head_count, HD)
    block_ids = (
        (slab_of[:, None] * group_count + group_index) * dev_blocks
        + jnp.arange(dev_blocks)[None, :]
    ).reshape(-1)
    member = jnp.any(
        (neighbours[:, :, None] == block_ids[None, None, :]) & listed_slot[:, :, None], axis=1
    )
    row_member = jnp.repeat(member, BLK, axis=0)
    partial_value, row_shift, group_total = attend_rows(
        slab_queries.reshape(-1, head_count, HD), row_member, near_keys, near_values, score_scale
    )
    received = (
        lax.all_to_all(partial_value[None], "ka", split_axis=1, concat_axis=0, tiled=True),
        lax.all_to_all(row_shift[None], "ka", split_axis=1, concat_axis=0, tiled=True),
        lax.all_to_all(group_total[None], "ka", split_axis=1, concat_axis=0, tiled=True),
    )
    group_out = received[0].reshape(group_count, dev_rows, head_count, HD).astype(jnp.float32)
    group_max = received[1].astype(jnp.float32)
    total_rounded = received[2].astype(jnp.float32)
    top_shift = jnp.max(group_max, axis=0, keepdims=True)
    weight_g = total_rounded * jnp.exp(group_max - top_shift)
    combined = (
        jnp.sum(weight_g[..., None] * group_out, axis=0) / jnp.sum(weight_g, axis=0)[..., None]
    )
    attended = combined.reshape(dev_rows, attn_width).astype(jnp.bfloat16)
    mixed = jnp.dot(
        attended,
        lax.all_gather(out_weight, ("pb", "ka"), axis=1, tiled=True),
        preferred_element_type=jnp.float32,
    )
    return mixed.astype(jnp.bfloat16)


def solution(mesh):
    return jax.shard_map(
        body,
        mesh=mesh,
        in_specs=(
            P(("pb", "ka"), None),
            P(("pb", "ka")),
            P("pb", None),
            P("pb"),
            P(("pb", "ka"), None),
            P(None, ("pb", "ka")),
        ),
        out_specs=P(("pb", "ka"), None),
        check_vma=False,
    )
```

profile of v0, /device:TPU:1, one launch (start us, length us, event | category | flops | bytes accessed | tf_op | source)
XLA Modules:
  0.0 470.9 jit_solution(14192227212871008691)
XLA Ops:
  6.5 0.7 all-gather.8.cloned.1.call-update
  7.3 0.7 compare_select_fusion
  8.0 1.6 gather_fusion
  9.5 0.7 compare_and_fusion
  10.2 124.0 %all-gather.8.cloned.1.call-done = bf16[512,2,1536]{2,1,0:T(2,128)(2,1)} async-done(((bf16[1,2,1536]{2,1,0:T(2,128)(2,1)}), bf16[512,2,1536]{2,1,0:T(2,128)(2,1)}) %all-gather.8.cloned.1.call-update) | async-done | bytes 3145744 | tf_op jit(solution)/shard_map/all_gather | solution.py:81
  134.2 6.3 %reshape.136 = bf16[1024,1536]{1,0:T(8,128)(2,1)S(1)} reshape(bf16[512,2,1536]{2,1,0:T(2,128)(2,1)} %all-gather.8.cloned.1.call-done) | data formatting | bytes 6291456
  140.6 1.6 convolution_convert_fusion
  142.2 0.7 copy-done.2
  142.9 0.7 slice.20
  143.6 1.0 slice.21
  144.6 3.1 collective-permute-start
  147.6 5.7 %collective-permute-start.1 = (bf16[128,1024]{1,0:T(8,128)(2,1)S(1)}, bf16[128,1024]{1,0:T(8,128)(2,1)S(1)}, u32[]{:S(2)}, u32[]{:S(2)}) collective-permute-start(bf16[128,1024]{1,0:T(8,128)(2,1)S(1)} %slice.21), channel_id=1, source_target_pairs={{16,0},{32,16},{48,32},{64,48},{80,64},{96,80},{112,96},{128,112},... | collective-permute-start | bytes 786440 | tf_op jit(solution)/shard_map/ppermute | solution.py:18
  153.5 0.2 and_reduce_fusion
  153.8 3.6 collective-permute-done
  157.4 0.9 collective-permute-done.1
  158.8 22.9 %all-gather.6.cloned.1.call-done = bf16[2048,512]{1,0:T(8,128)(2,1)} async-done(((bf16[128,512]{1,0:T(8,128)(2,1)}), bf16[2048,512]{1,0:T(8,128)(2,1)}) %all-gather.6.cloned.1.call-update) | async-done | bytes 2097168 | tf_op jit(solution)/shard_map/all_gather | solution.py:94
  181.7 6.2 %reshape.139 = bf16[4,512,8,64]{3,2,1,0:T(8,128)(2,1)} reshape(bf16[2048,512]{1,0:T(8,128)(2,1)} %all-gather.6.cloned.1.call-done) | data formatting | bytes 4194304 | tf_op jit(solution)/shard_map/reshape;reshape | solution.py:62
  187.9 5.5 %copy.79 = bf16[4,512,8,64]{1,3,2,0:T(8,128)(2,1)} copy(bf16[4,512,8,64]{3,2,1,0:T(8,128)(2,1)} %reshape.139) | data formatting | bytes 4194304 | tf_op jit(solution)/shard_map/while | solution.py:59
  193.3 24.9 %while.14 = (s32[]{:T(128)}, bf16[4,512,512]{2,1,0:T(8,128)(2,1)}, bf16[4,512,8]{1,2,0:T(8,128)(2,1)S(1)}, bf16[4,512,8]{1,2,0:T(8,128)(2,1)S(1)}, pred[4,512,3]...) while((s32[]{:T(128)}, bf16[4,512,512]{2,1,0:T(8,128)(2,1)}, ...), condition=%wide.region_4.5_spmd, body=%wide.region_1.4_spmd.sunk | while | flops 420753408 | bytes 23795300 | solution.py:59
  193.4 2.2 select_reduce_fusion.2
  195.6 1.3 fusion.40
  197.0 1.5 select_convert_fusion.2
  198.5 0.2 copy.99
  198.7 0.8 constant_dynamic-update-slice_fusion.2
  199.6 2.2 select_reduce_fusion.2
  201.8 1.3 fusion.40
  203.2 1.5 select_convert_fusion.2
  204.7 0.2 copy.99
  204.9 0.9 constant_dynamic-update-slice_fusion.2
  205.8 2.2 select_reduce_fusion.2
  208.0 1.3 fusion.40
  209.4 1.5 select_convert_fusion.2
  211.1 0.8 constant_dynamic-update-slice_fusion.2
  212.0 2.2 select_reduce_fusion.2
  214.2 1.3 fusion.40
  215.6 1.5 select_convert_fusion.2
  217.3 0.9 constant_dynamic-update-slice_fusion.2
  218.2 0.7 copy.82
  218.9 0.5 broadcast.127
  219.4 12.2 %reduce.6 = bf16[2048,8]{1,0:T(8,128)(2,1)} reduce(bf16[2048,1,8]{2,1,0:T(2,128)(2,1)S(1)} %bitcast.101, bf16[]{:T(256)} %broadcast.127), dimensions={1}, to_apply=%bitcast.57.reduce_sub_computation | reduce | bytes 65538
  231.7 2.2 reshape.144
  233.8 4.9 %all-to-all-start.1 = ((bf16[16,2,512]{2,1,0:T(2,128)(2,1)}), bf16[16,2,512]{2,1,0:T(2,128)(2,1)S(1)}, u32[]{:S(2)}, u32[]{:S(2)}) async-start(bf16[16,2,512]{2,1,0:T(2,128)(2,1)} %reshape.144), calls=%async_computation.1 | async-start | bytes 65536 | tf_op jit(solution)/shard_map/all_to_all | solution.py:110
  238.7 0.7 copy.80
  239.5 12.2 %reduce.7 = bf16[2048,8]{1,0:T(8,128)(2,1)} reduce(bf16[2048,1,8]{2,1,0:T(2,128)(2,1)S(1)} %bitcast.102, bf16[]{:T(256)} %broadcast.127), dimensions={1}, to_apply=%bitcast.55.reduce_sub_computation | reduce | bytes 65538
  251.7 2.2 reshape.142
  253.9 7.2 %all-to-all-start = ((bf16[16,2,512]{2,1,0:T(2,128)(2,1)}), bf16[16,2,512]{2,1,0:T(2,128)(2,1)S(1)}, u32[]{:S(2)}, u32[]{:S(2)}) async-start(bf16[16,2,512]{2,1,0:T(2,128)(2,1)} %reshape.142), calls=%async_computation | async-start | bytes 65536 | tf_op jit(solution)/shard_map/all_to_all | solution.py:111
  261.1 18.5 %copy.97 = bf16[1,2048,512]{2,0,1:T(2,128)(2,1)} copy(bf16[1,2048,512]{2,1,0:T(8,128)(2,1)S(1)} %bitcast.105) | data formatting | bytes 4194304 | tf_op jit(solution)/shard_map/broadcast_in_dim;reshape | solution.py:109
  279.7 14.0 %reduce.5 = bf16[2048,512]{1,0:T(8,128)(2,1)S(1)} reduce(bf16[2048,1,512]{2,1,0:T(2,128)(2,1)} %bitcast.95, bf16[]{:T(256)} %broadcast.127), dimensions={1}, to_apply=%bitcast.69.reduce_sub_computation | reduce | bytes 4194306
  293.7 2.8 reshape.140
  296.5 7.2 %all-to-all-start.2 = ((bf16[16,2,32768]{2,1,0:T(2,128)(2,1)}), bf16[16,2,32768]{2,1,0:T(2,128)(2,1)S(1)}, u32[]{:S(2)}, u32[]{:S(2)}) async-start(bf16[16,2,32768]{2,1,0:T(2,128)(2,1)} %reshape.140), calls=%async_computation.2 | async-start | bytes 4194304 | tf_op jit(solution)/shard_map/all_to_all | solution.py:109
  303.7 0.3 all-gather.10.cloned.1.call-start
  304.0 0.4 all-gather.10.cloned.1.call-update
  304.4 126.7 %all-gather.10.cloned.1.call-done = bf16[512,2,512]{2,1,0:T(2,128)(2,1)} async-done(((bf16[1,2,512]{2,1,0:T(2,128)(2,1)}), bf16[512,2,512]{2,1,0:T(2,128)(2,1)}) %all-gather.10.cloned.1.call-update) | async-done | bytes 1048592 | tf_op jit(solution)/shard_map/all_gather | solution.py:124
  431.1 1.5 reshape.138
  432.6 2.5 reshape.145
  435.1 2.2 copy.83
  437.4 2.5 reshape.143
  439.9 2.2 copy.81
  442.2 6.8 %reshape.141 = bf16[2048,1,512]{2,1,0:T(2,128)(2,1)} reshape(bf16[16,2,32768]{2,1,0:T(2,128)(2,1)S(1)} %all-to-all-done.2) | data formatting | bytes 4194304
  449.0 4.6 copy_convert_fusion
  453.6 5.5 %copy.88 = f32[1,2048,512]{1,2,0:T(8,128)} copy(f32[1,2048,512]{2,1,0:T(8,128)} %copy_convert_fusion) | data formatting | bytes 8388608 | tf_op jit(solution)/shard_map/convert_element_type | solution.py:113
  459.1 3.1 copy.94
  462.2 1.0 multiply_reduce_fusion
  463.2 1.2 convolution_convert_fusion.1
  (59 shorter events, 1.7 us)
Async XLA Ops:
  6.5 1.4 copy-start
  6.5 127.7 %all-gather.8.cloned.1.call-start = ((), (), s32[]{:S(2)}) async-start(), calls=%async_computation.4 | async-start | bytes 3151872 | tf_op jit(solution)/shard_map/all_gather | solution.py:81
  7.3 174.4 %all-gather.6.cloned.1.call-start = ((), (), s32[]{:S(2)}) async-start(), calls=%async_computation.3 | async-start | bytes 2228224 | tf_op jit(solution)/shard_map/all_gather | solution.py:94
  10.2 143.2 %copy-start.4 = (s32[16]{0:T(128)S(1)}, s32[16]{0:T(128)}, u32[]{:S(2)}) copy-start(s32[16]{0:T(128)} %param.11) | copy-start | bytes 196
  10.2 143.3 %copy-start.3 = (s32[16,24]{1,0:T(8,128)S(1)}, s32[16,24]{1,0:T(8,128)}, u32[]{:S(2)}) copy-start(s32[16,24]{1,0:T(8,128)} %param.10) | copy-start | bytes 4612
  142.2 0.7 copy-start.2
  144.6 12.8 %collective-permute-start = (bf16[128,1024]{1,0:T(8,128)(2,1)S(1)}, bf16[128,1024]{1,0:T(8,128)(2,1)S(1)}, u32[]{:S(2)}, u32[]{:S(2)}) collective-permute-start(bf16[128,1024]{1,0:T(8,128)(2,1)S(1)} %slice.21), channel_id=1, source_target_pairs={{0,16},{16,32},{32,48},{48,64},{64,80},{80,96},{96,112},{112,128},... | collective-permute-start | bytes 786440 | tf_op jit(solution)/shard_map/ppermute | solution.py:17
  147.6 10.6 %collective-permute-start.1 = (bf16[128,1024]{1,0:T(8,128)(2,1)S(1)}, bf16[128,1024]{1,0:T(8,128)(2,1)S(1)}, u32[]{:S(2)}, u32[]{:S(2)}) collective-permute-start(bf16[128,1024]{1,0:T(8,128)(2,1)S(1)} %slice.21), channel_id=1, source_target_pairs={{16,0},{32,16},{48,32},{64,48},{80,64},{96,80},{112,96},{128,112},... | collective-permute-start | bytes 786440 | tf_op jit(solution)/shard_map/ppermute | solution.py:18
  218.2 42.9 %copy-start.1 = (bf16[4,512,512]{2,1,0:T(8,128)(2,1)S(1)}, bf16[4,512,512]{2,1,0:T(8,128)(2,1)}, u32[]{:S(2)}) copy-start(bf16[4,512,512]{2,1,0:T(8,128)(2,1)} %get-tuple-element.51) | copy-start | bytes 6291460
  233.8 20.1 %all-to-all-start.1 = ((bf16[16,2,512]{2,1,0:T(2,128)(2,1)}), bf16[16,2,512]{2,1,0:T(2,128)(2,1)S(1)}, u32[]{:S(2)}, u32[]{:S(2)}) async-start(bf16[16,2,512]{2,1,0:T(2,128)(2,1)} %reshape.144), calls=%async_computation.1 | async-start | bytes 65536 | tf_op jit(solution)/shard_map/all_to_all | solution.py:110
  253.9 42.6 %all-to-all-start = ((bf16[16,2,512]{2,1,0:T(2,128)(2,1)}), bf16[16,2,512]{2,1,0:T(2,128)(2,1)S(1)}, u32[]{:S(2)}, u32[]{:S(2)}) async-start(bf16[16,2,512]{2,1,0:T(2,128)(2,1)} %reshape.142), calls=%async_computation | async-start | bytes 65536 | tf_op jit(solution)/shard_map/all_to_all | solution.py:111
  296.5 145.7 %all-to-all-start.2 = ((bf16[16,2,32768]{2,1,0:T(2,128)(2,1)}), bf16[16,2,32768]{2,1,0:T(2,128)(2,1)S(1)}, u32[]{:S(2)}, u32[]{:S(2)}) async-start(bf16[16,2,32768]{2,1,0:T(2,128)(2,1)} %reshape.140), calls=%async_computation.2 | async-start | bytes 4194304 | tf_op jit(solution)/shard_map/all_to_all | solution.py:109
  303.7 127.5 %all-gather.10.cloned.1.call-start = ((), (), s32[]{:S(2)}) async-start(), calls=%async_computation.5 | async-start | bytes 1050624 | tf_op jit(solution)/shard_map/all_gather | solution.py:124
Sparse Core Ops, SparseCore 0:
  11.5 122.6 all-gather.7
  143.7 37.9 all-gather.5
  308.7 122.4 all-gather.9
where the time goes:
time: 472 us; the launch traced here: 471 us
  waiting for transfers between devices  279 us (59%)
  local copies, waits for them, and re-layouts  80.9 us (17%)
  other arithmetic  51.1 us (11%)
  starting transfers between devices  28.5 us (6%)
  matrix products  17.6 us (4%)
  between operations  13.3 us (3%)
    all_gather x1, waiting for transfers between devices, body(): lax.all_gather(out_weight, ('pb', 'ka'), axis=1, tiled=True)  127 us
    all_gather x1, waiting for transfers between devices, body(): lax.all_gather(qkv_weight, ('pb', 'ka'), axis=0, tiled=True)  124 us
    unnamed x3, other arithmetic  38.5 us
    unnamed x20, local copies, waits for them, and re-layouts  31.1 us
    all_gather x1, waiting for transfers between devices, body(): slab_queries = lax.all_gather(own_queries, 'ka', axis=0, tiled=True)  22.9 us
    another operation x1, local copies, waits for them, and re-layouts, body(): partial_value[None]  18.5 us
  transfers between devices with their start and end apart: 8, of which 5 were waited for; matrix products, arithmetic and copies ran while one was open for 14% of the time, Pallas kernels for 0%

commit v1 on v0

--- a/solution.py
+++ b/solution.py
@@ -5,6 +5,14 @@
 
 HD = 64
 BLK = 128
+
+
+def test_trees(xs, lane_axis, at_axis):
+    log = []
+    for _ in range(lax.axis_size(lane_axis)):
+        log.append(xs)
+    now = jnp.concatenate(lax.all_to_all(jnp.stack(log), lane_axis, 0, 0), axis=at_axis)
+    return now
 
 
 def padded(array, sides, width):
@@ -91,7 +99,7 @@
     dev_blocks = dev_rows // BLK
     slab_of = (slab_index + jnp.arange(3) - 1) % slab_count
     listed_slot = jnp.arange(neighbours.shape[1])[None, :] < counts[:, None]
-    slab_queries = lax.all_gather(own_queries, "ka", axis=0, tiled=True)
+    slab_queries = test_trees(own_queries, "ka", 0)
     near_keys = near[:, :attn_width].reshape(3 * dev_rows, head_count, HD)
     near_values = near[:, attn_width:].reshape(3 * dev_rows, head_count, HD)
     block_ids = (

time: 472 us -> 489 us (1.036)
  waiting for transfers between devices: 279 us -> 289 us
    all_to_all x0 -> x1, waiting for transfers between devices: none -> 32 us  [test_trees(): lax.all_to_all(jnp.stack(log), lane_axis, 0, 0)]
    all_gather x1 -> x0, waiting for transfers between devices: 22.9 us -> none  [body(): slab_queries = lax.all_gather(own_queries, 'ka', axis=0, tiled=True)]
    unnamed x20 -> x22, local copies, waits for them, and re-layouts: 31.1 us -> 31.1 us
where the time goes in v1:
time: 489 us; the launch traced here: 488 us
  waiting for transfers between devices  289 us (59%)
  local copies, waits for them, and re-layouts  79.3 us (16%)
  other arithmetic  51.1 us (10%)
  starting transfers between devices  32.5 us (7%)
  matrix products  21.8 us (4%)
  between operations  13.6 us (3%)
    all_gather x1, waiting for transfers between devices, body(): lax.all_gather(out_weight, ('pb', 'ka'), axis=1, tiled=True)  127 us
    all_gather x1, waiting for transfers between devices, body(): lax.all_gather(qkv_weight, ('pb', 'ka'), axis=0, tiled=True)  124 us
    unnamed x3, other arithmetic  38.5 us
    all_to_all x1, waiting for transfers between devices, test_trees(): lax.all_to_all(jnp.stack(log), lane_axis, 0, 0)  32 us
    unnamed x22, local copies, waits for them, and re-layouts  31.1 us
    another operation x1, local copies, waits for them, and re-layouts, body(): partial_value[None]  18.5 us
    dot_general x4, matrix products, attend(): jnp.einsum('hqk,khd->qhd', soft_weights.astype(jnp.bfloat16), near_values...  10.2 us
  transfers between devices with their start and end apart: 8, of which 5 were waited for; matrix products, arithmetic and copies ran while one was open for 14% of the time, Pallas kernels for 0%

profile of v1, /device:TPU:1, one launch (start us, length us, event | category | flops | bytes accessed | tf_op | source)
XLA Modules:
  0.0 487.7 jit_solution(14466848398246503076)
XLA Ops:
  6.5 0.7 all-gather.5.cloned.1.call-update
  7.3 0.7 compare_select_fusion
  7.9 1.6 gather_fusion
  9.5 0.7 compare_and_fusion
  10.2 124.1 %all-gather.5.cloned.1.call-done = bf16[512,2,1536]{2,1,0:T(2,128)(2,1)} async-done(((bf16[1,2,1536]{2,1,0:T(2,128)(2,1)}), bf16[512,2,1536]{2,1,0:T(2,128)(2,1)}) %all-gather.5.cloned.1.call-update) | async-done | bytes 3145744 | tf_op jit(solution)/shard_map/all_gather | solution.py:89
  134.2 6.3 %reshape.138 = bf16[1024,1536]{1,0:T(8,128)(2,1)S(1)} reshape(bf16[512,2,1536]{2,1,0:T(2,128)(2,1)} %all-gather.5.cloned.1.call-done) | data formatting | bytes 6291456
  140.6 1.6 convolution_convert_fusion
  142.2 0.7 copy-done.2
  143.1 1.8 stack.2
  144.8 4.4 all-to-all-start
  149.3 2.8 collective-permute-start
  152.1 5.9 %collective-permute-start.1 = (bf16[128,1024]{1,0:T(8,128)(2,1)S(1)}, bf16[128,1024]{1,0:T(8,128)(2,1)S(1)}, u32[]{:S(2)}, u32[]{:S(2)}) collective-permute-start(bf16[128,1024]{1,0:T(8,128)(2,1)S(1)} %slice.21), channel_id=1, source_target_pairs={{16,0},{32,16},{48,32},{64,48},{80,64},{96,80},{112,96},{128,112},... | collective-permute-start | bytes 786440 | tf_op jit(solution)/shard_map/ppermute | solution.py:26
  158.4 4.0 collective-permute-done
  162.4 0.9 collective-permute-done.1
  163.3 0.8 fusion.26
  164.1 1.2 copy.80
  165.3 0.9 copy.81
  166.2 32.0 %all-to-all-done = bf16[16,128,512]{1,2,0:T(8,128)(2,1)S(1)} async-done(((bf16[16,128,512]{1,2,0:T(8,128)(2,1)}), bf16[16,128,512]{1,2,0:T(8,128)(2,1)S(1)}, u32[]{:S(2)}, u32[]{:S(2)}) %all-to-all-start) | async-done | bytes 2097184 | tf_op jit(solution)/shard_map/all_to_all | solution.py:14
  198.2 2.7 copy.79
  200.9 2.7 reshape_reshape_reshape.3
  203.7 1.8 copy.83
  205.5 29.0 %while.14 = (s32[]{:T(128)}, bf16[4,512,512]{2,1,0:T(8,128)(2,1)}, bf16[4,512,8]{1,2,0:T(8,128)(2,1)S(1)}, bf16[4,512,8]{1,2,0:T(8,128)(2,1)S(1)}, pred[4,512,3]...) while((s32[]{:T(128)}, bf16[4,512,512]{2,1,0:T(8,128)(2,1)}, ...), condition=%wide.region_4.5_spmd, body=%wide.region_1.4_spmd.sunk | while | flops 420753408 | bytes 23795300 | solution.py:67
  205.6 2.2 select_reduce_fusion.2
  207.8 1.3 fusion.40
  209.1 2.5 select_convert_fusion.2
  211.9 0.8 constant_dynamic-update-slice_fusion.2
  212.8 2.2 select_reduce_fusion.2
  215.0 1.3 fusion.40
  216.4 2.5 select_convert_fusion.2
  219.1 0.8 constant_dynamic-update-slice_fusion.2
  220.0 2.2 select_reduce_fusion.2
  222.3 1.3 fusion.40
  223.6 2.5 select_convert_fusion.2
  226.4 0.8 constant_dynamic-update-slice_fusion.2
  227.3 2.2 select_reduce_fusion.2
  229.5 1.3 fusion.40
  230.9 2.5 select_convert_fusion.2
  233.6 0.8 constant_dynamic-update-slice_fusion.2
  234.5 0.7 copy.86
  235.2 0.5 broadcast.129
  235.7 12.2 %reduce.6 = bf16[2048,8]{1,0:T(8,128)(2,1)} reduce(bf16[2048,1,8]{2,1,0:T(2,128)(2,1)S(1)} %bitcast.103, bf16[]{:T(256)} %broadcast.129), dimensions={1}, to_apply=%bitcast.59.reduce_sub_computation | reduce | bytes 65538
  247.9 2.2 reshape.145
  250.1 5.0 %all-to-all-start.2 = ((bf16[16,2,512]{2,1,0:T(2,128)(2,1)}), bf16[16,2,512]{2,1,0:T(2,128)(2,1)S(1)}, u32[]{:S(2)}, u32[]{:S(2)}) async-start(bf16[16,2,512]{2,1,0:T(2,128)(2,1)} %reshape.145), calls=%async_computation.2 | async-start | bytes 65536 | tf_op jit(solution)/shard_map/all_to_all | solution.py:118
  255.1 0.7 copy.84
  255.8 12.2 %reduce.7 = bf16[2048,8]{1,0:T(8,128)(2,1)} reduce(bf16[2048,1,8]{2,1,0:T(2,128)(2,1)S(1)} %bitcast.104, bf16[]{:T(256)} %broadcast.129), dimensions={1}, to_apply=%bitcast.57.reduce_sub_computation | reduce | bytes 65538
  268.1 2.2 reshape.143
  270.3 7.2 %all-to-all-start.1 = ((bf16[16,2,512]{2,1,0:T(2,128)(2,1)}), bf16[16,2,512]{2,1,0:T(2,128)(2,1)S(1)}, u32[]{:S(2)}, u32[]{:S(2)}) async-start(bf16[16,2,512]{2,1,0:T(2,128)(2,1)} %reshape.143), calls=%async_computation.1 | async-start | bytes 65536 | tf_op jit(solution)/shard_map/all_to_all | solution.py:119
  277.5 18.5 %copy.99 = bf16[1,2048,512]{2,0,1:T(2,128)(2,1)} copy(bf16[1,2048,512]{2,1,0:T(8,128)(2,1)S(1)} %bitcast.107) | data formatting | bytes 4194304 | tf_op jit(solution)/shard_map/broadcast_in_dim;reshape | solution.py:117
  296.0 14.0 %reduce.5 = bf16[2048,512]{1,0:T(8,128)(2,1)S(1)} reduce(bf16[2048,1,512]{2,1,0:T(2,128)(2,1)} %bitcast.97, bf16[]{:T(256)} %broadcast.129), dimensions={1}, to_apply=%bitcast.71.reduce_sub_computation | reduce | bytes 4194306
  310.0 2.8 reshape.141
  312.8 7.2 %all-to-all-start.3 = ((bf16[16,2,32768]{2,1,0:T(2,128)(2,1)}), bf16[16,2,32768]{2,1,0:T(2,128)(2,1)S(1)}, u32[]{:S(2)}, u32[]{:S(2)}) async-start(bf16[16,2,32768]{2,1,0:T(2,128)(2,1)} %reshape.141), calls=%async_computation.3 | async-start | bytes 4194304 | tf_op jit(solution)/shard_map/all_to_all | solution.py:117
  320.1 0.7 all-gather.7.cloned.1.call-update
  320.8 126.8 %all-gather.7.cloned.1.call-done = bf16[512,2,512]{2,1,0:T(2,128)(2,1)} async-done(((bf16[1,2,512]{2,1,0:T(2,128)(2,1)}), bf16[512,2,512]{2,1,0:T(2,128)(2,1)}) %all-gather.7.cloned.1.call-update) | async-done | bytes 1048592 | tf_op jit(solution)/shard_map/all_gather | solution.py:132
  447.6 1.5 reshape.140
  449.1 2.5 reshape.146
  451.6 2.2 copy.87
  453.9 2.5 reshape.144
  456.4 2.2 copy.85
  458.7 6.8 %reshape.142 = bf16[2048,1,512]{2,1,0:T(2,128)(2,1)} reshape(bf16[16,2,32768]{2,1,0:T(2,128)(2,1)S(1)} %all-to-all-done.3) | data formatting | bytes 4194304
  465.5 4.6 copy_convert_fusion
  470.1 5.5 %copy.92 = f32[1,2048,512]{1,2,0:T(8,128)} copy(f32[1,2048,512]{2,1,0:T(8,128)} %copy_convert_fusion) | data formatting | bytes 8388608 | tf_op jit(solution)/shard_map/convert_element_type | solution.py:121
  475.6 3.1 copy.96
  478.7 1.0 multiply_reduce_fusion
  479.7 1.2 convolution_convert_fusion.1
  (63 shorter events, 2.0 us)
Async XLA Ops:
  6.5 1.4 copy-start
  6.5 127.7 %all-gather.5.cloned.1.call-start = ((), (), s32[]{:S(2)}) async-start(), calls=%async_computation.4 | async-start | bytes 3151872 | tf_op jit(solution)/shard_map/all_gather | solution.py:89
  142.2 0.8 copy-start.2
  142.9 15.0 %copy-start.5 = (s32[16]{0:T(128)S(1)}, s32[16]{0:T(128)}, u32[]{:S(2)}) copy-start(s32[16]{0:T(128)} %param.11) | copy-start | bytes 196
  142.9 15.1 %copy-start.4 = (s32[16,24]{1,0:T(8,128)S(1)}, s32[16,24]{1,0:T(8,128)}, u32[]{:S(2)}) copy-start(s32[16,24]{1,0:T(8,128)} %param.10) | copy-start | bytes 4612
  142.9 6.3 %copy-start.3 = (bf16[128,1536]{1,0:T(8,128)(2,1)S(1)}, bf16[128,1536]{1,0:T(8,128)(2,1)}, u32[]{:S(2)}) copy-start(bf16[128,1536]{1,0:T(8,128)(2,1)} %copy-done.2) | copy-start | bytes 1179652
  144.8 53.4 %all-to-all-start = ((bf16[16,128,512]{1,2,0:T(8,128)(2,1)}), bf16[16,128,512]{1,2,0:T(8,128)(2,1)S(1)}, u32[]{:S(2)}, u32[]{:S(2)}) async-start(bf16[16,128,512]{1,2,0:T(8,128)(2,1)} %stack.2), calls=%async_computation | async-start | bytes 4194304 | tf_op jit(solution)/shard_map/all_to_all | solution.py:14
  149.3 13.1 %collective-permute-start = (bf16[128,1024]{1,0:T(8,128)(2,1)S(1)}, bf16[128,1024]{1,0:T(8,128)(2,1)S(1)}, u32[]{:S(2)}, u32[]{:S(2)}) collective-permute-start(bf16[128,1024]{1,0:T(8,128)(2,1)S(1)} %slice.21), channel_id=1, source_target_pairs={{0,16},{16,32},{32,48},{48,64},{64,80},{80,96},{96,112},{112,128},... | collective-permute-start | bytes 786440 | tf_op jit(solution)/shard_map/ppermute | solution.py:25
  152.1 11.2 %collective-permute-start.1 = (bf16[128,1024]{1,0:T(8,128)(2,1)S(1)}, bf16[128,1024]{1,0:T(8,128)(2,1)S(1)}, u32[]{:S(2)}, u32[]{:S(2)}) collective-permute-start(bf16[128,1024]{1,0:T(8,128)(2,1)S(1)} %slice.21), channel_id=1, source_target_pairs={{16,0},{32,16},{48,32},{64,48},{80,64},{96,80},{112,96},{128,112},... | collective-permute-start | bytes 786440 | tf_op jit(solution)/shard_map/ppermute | solution.py:26
  234.5 43.0 %copy-start.1 = (bf16[4,512,512]{2,1,0:T(8,128)(2,1)S(1)}, bf16[4,512,512]{2,1,0:T(8,128)(2,1)}, u32[]{:S(2)}) copy-start(bf16[4,512,512]{2,1,0:T(8,128)(2,1)} %get-tuple-element.51) | copy-start | bytes 6291460
  250.1 20.1 %all-to-all-start.2 = ((bf16[16,2,512]{2,1,0:T(2,128)(2,1)}), bf16[16,2,512]{2,1,0:T(2,128)(2,1)S(1)}, u32[]{:S(2)}, u32[]{:S(2)}) async-start(bf16[16,2,512]{2,1,0:T(2,128)(2,1)} %reshape.145), calls=%async_computation.2 | async-start | bytes 65536 | tf_op jit(solution)/shard_map/all_to_all | solution.py:118
  270.3 42.6 %all-to-all-start.1 = ((bf16[16,2,512]{2,1,0:T(2,128)(2,1)}), bf16[16,2,512]{2,1,0:T(2,128)(2,1)S(1)}, u32[]{:S(2)}, u32[]{:S(2)}) async-start(bf16[16,2,512]{2,1,0:T(2,128)(2,1)} %reshape.143), calls=%async_computation.1 | async-start | bytes 65536 | tf_op jit(solution)/shard_map/all_to_all | solution.py:119
  312.8 145.8 %all-to-all-start.3 = ((bf16[16,2,32768]{2,1,0:T(2,128)(2,1)}), bf16[16,2,32768]{2,1,0:T(2,128)(2,1)S(1)}, u32[]{:S(2)}, u32[]{:S(2)}) async-start(bf16[16,2,32768]{2,1,0:T(2,128)(2,1)} %reshape.141), calls=%async_computation.3 | async-start | bytes 4194304 | tf_op jit(solution)/shard_map/all_to_all | solution.py:117
  320.1 127.6 %all-gather.7.cloned.1.call-start = ((), (), s32[]{:S(2)}) async-start(), calls=%async_computation.5 | async-start | bytes 1050624 | tf_op jit(solution)/shard_map/all_gather | solution.py:132
Sparse Core Ops, SparseCore 0:
  11.5 122.6 all-gather.4
  325.1 122.5 all-gather.6
